TPU v7x, 256 devices: a whole 4x4x8 slice. The times are simulated.
256 devices in a mesh: ctx: 32 (over z, y_lo, core), head: 8 (over x, y_hi).
Axes of the slice: x: 4, y: 4 (y_hi: 2, y_lo: 2; y = y_hi * 2 + y_lo), z: 8, core: 2. Of those that a mesh axis runs over, the one named last changes fastest.
Arguments:
- queries: bfloat16 [4096, 8192], P('ctx', 'head'), may hold values from -5 to 5
- key_rows: bfloat16 [4096, 1024], P('ctx', 'head'), may hold values from -5 to 5
- value_rows: bfloat16 [4096, 1024], P('ctx', 'head'), may hold values from -6 to 6
- query_tangent: bfloat16 [4096, 8192], P('ctx', 'head'), may hold values from -16 to 16
- key_tangent: bfloat16 [4096, 1024], P('ctx', 'head'), may hold values from -3 to 3
- value_tangent: bfloat16 [4096, 1024], P('ctx', 'head'), may hold values from -6 to 6
- block_order: int32 [32], replicated, may hold values from 0 to 31, each once
Outputs:
- attended: bfloat16 [4096, 8192], P('ctx', 'head')
- probe_out: bfloat16 [4096, 8192], P('ctx', 'head')
- probe_norm: float32 [], replicated
Inputs may be any that keep to these rules, and one draw needn't show every extreme that they name: `block_order`: each block index appears exactly once.
All inputs are finite; a program needn't handle non-finite values.
Results may differ from a plain program's by a relative error of at most 0.025.
Values may be sent and summed in bfloat16 or wider, within the bound.
No kernel may reach another device: no remote copies, remote signals or barrier semaphores. Data moves between devices by JAX's collectives and lax.ppermute only.
A program may use at most 64 MiB of HBM per device.

v0:
```python
import math
import jax
import jax.numpy as jnp
from jax import lax
from jax.sharding import PartitionSpec as P

HEAD_DIM = 128
floor_score = -1e30


def lookup(table, entries):
    return jnp.sum(jnp.where(entries[..., None] == jnp.arange(table.shape[0]), table, 0), axis=-1)


def attend(
    query_block, qtan_block, key_block, value_block, ktan_block, vtan_block, visible, running
):
    factor = 1.0 / math.sqrt(query_block.shape[-1])
    scores = (
        jnp.einsum("tghd,sgd->tghs", query_block, key_block, preferred_element_type=jnp.float32)
        * factor
    )
    scores = jnp.where(visible[:, None, None, :], scores, floor_score)
    top_old, totals_old, drifts_old, numer_old, tangent_old = running
    top_new = jnp.maximum(top_old, jnp.max(scores, axis=-1))
    shrink = jnp.exp(top_old - top_new)
    weights = jnp.exp(scores - top_new[..., None])
    weights = jnp.where(visible[:, None, None, :], weights, 0.0)
    slopes = (
        jnp.einsum("tghd,sgd->tghs", qtan_block, key_block, preferred_element_type=jnp.float32)
        + jnp.einsum("tghd,sgd->tghs", query_block, ktan_block, preferred_element_type=jnp.float32)
    ) * factor
    tilted = weights * slopes
    totals = shrink * totals_old + jnp.sum(weights, axis=-1)
    drifts = shrink * drifts_old + jnp.sum(tilted, axis=-1)
    low_weights = weights.astype(jnp.bfloat16)
    low_tilted = tilted.astype(jnp.bfloat16)
    numerator = shrink[..., None] * numer_old + jnp.einsum(
        "tghs,sgd->tghd", low_weights, value_block, preferred_element_type=jnp.float32
    )
    tangent_num = (
        shrink[..., None] * tangent_old
        + jnp.einsum("tghs,sgd->tghd", low_tilted, value_block, preferred_element_type=jnp.float32)
        + jnp.einsum("tghs,sgd->tghd", low_weights, vtan_block, preferred_element_type=jnp.float32)
    )
    return (top_new, totals, drifts, numerator, tangent_num)


def empty_sums(q_four):
    stat_shape = q_four.shape[:3]
    return (
        jnp.full(stat_shape, floor_score, jnp.float32),
        jnp.zeros(stat_shape, jnp.float32),
        jnp.zeros(stat_shape, jnp.float32),
        jnp.zeros(q_four.shape, jnp.float32),
        jnp.zeros(q_four.shape, jnp.float32),
    )


def make_fold(q_four, dq_four, query_pos, block_order, block_rows):

    def fold_keys(running, pieces, start):
        length = pieces[0].shape[0]
        span = 512

        def sweep(sweep_no, held):
            offset = sweep_no * span
            k_part = lax.dynamic_slice_in_dim(pieces[0], offset, span, 0)
            v_part = lax.dynamic_slice_in_dim(pieces[1], offset, span, 0)
            dk_part = lax.dynamic_slice_in_dim(pieces[2], offset, span, 0)
            dv_part = lax.dynamic_slice_in_dim(pieces[3], offset, span, 0)
            key_index = offset + jnp.arange(span, dtype=jnp.int32)
            key_pos = (
                lookup(block_order, key_index // block_rows) * block_rows + key_index % block_rows
            )
            visible = key_pos[None, :] <= query_pos[:, None]
            return attend(q_four, dq_four, k_part, v_part, dk_part, dv_part, visible, held)

        return lax.fori_loop(0, length // span, sweep, running)

    return fold_keys


def finish(final, width):
    top_final, totals, drifts, numerator, tangent_num = final
    rows = numerator.shape[0]
    attended = (numerator / totals[..., None]).astype(jnp.bfloat16).reshape(rows, width)
    probe = (tangent_num - numerator * drifts[..., None] / totals[..., None]) / totals[..., None]
    square_sum = jnp.sum(probe * probe)
    probe_out = probe.astype(jnp.bfloat16).reshape(rows, width)
    return (attended, probe_out, square_sum)


def shards(queries, key_rows, value_rows, query_tangent, key_tangent, value_tangent, block_order):
    row_count = queries.shape[0]
    width = queries.shape[1]
    groups = key_rows.shape[1] // HEAD_DIM
    shares = width // key_rows.shape[1]
    q_four = queries.reshape(row_count, groups, shares, HEAD_DIM)
    dq_four = query_tangent.reshape(row_count, groups, shares, HEAD_DIM)
    k_three = key_rows.reshape(row_count, groups, HEAD_DIM)
    v_three = value_rows.reshape(row_count, groups, HEAD_DIM)
    dk_three = key_tangent.reshape(row_count, groups, HEAD_DIM)
    dv_three = value_tangent.reshape(row_count, groups, HEAD_DIM)
    empty = empty_sums(q_four)
    count = lax.axis_size("ctx")
    own_index = lax.axis_index("ctx")
    own_block = lookup(block_order, own_index)
    local_rows = jnp.arange(row_count, dtype=jnp.int32)
    query_pos = own_block * row_count + local_rows
    fold_keys = make_fold(q_four, dq_four, query_pos, block_order, row_count)
    final = fold_keys(
        empty,
        (
            lax.all_gather(k_three, "ctx", axis=0, tiled=True),
            lax.all_gather(v_three, "ctx", axis=0, tiled=True),
            lax.all_gather(dk_three, "ctx", axis=0, tiled=True),
            lax.all_gather(dv_three, "ctx", axis=0, tiled=True),
        ),
        jnp.int32(0),
    )
    attended, probe_out, square_sum = finish(final, width)
    total_squares = lax.psum(square_sum, ("ctx", "head"))
    entries = row_count * width * count * lax.axis_size("head")
    probe_norm = jnp.sqrt(total_squares / entries)
    return (attended, probe_out, probe_norm)


def solution(mesh):
    in_specs = (
        P("ctx", "head"),
        P("ctx", "head"),
        P("ctx", "head"),
        P("ctx", "head"),
        P("ctx", "head"),
        P("ctx", "head"),
        P(),
    )
    out_specs = (P("ctx", "head"), P("ctx", "head"), P())
    return jax.shard_map(shards, mesh=mesh, in_specs=in_specs, out_specs=out_specs, check_vma=False)
```

profile of v0, /device:TPU:1, one launch (start us, length us, event | category | flops | bytes accessed | tf_op | source)
XLA Modules:
  0.0 435.9 jit_solution(5790193779577094986)
XLA Ops:
  7.2 0.7 all-gather.9.cloned.1.call-update
  8.0 0.7 all-gather.11.cloned.1.call-update
  8.7 1.5 copy.33
  10.3 1.5 copy.34
  11.8 1.1 copy.31
  13.1 1.1 copy.32
  14.5 0.6 fusion.42
  15.7 61.9 %all-gather.9.cloned.1.call-done = bf16[4096,128]{1,0:T(8,128)(2,1)} async-done(((bf16[128,128]{1,0:T(8,128)(2,1)}), bf16[4096,128]{1,0:T(8,128)(2,1)}) %all-gather.9.cloned.1.call-update) | async-done | bytes 1048592 | tf_op jit(solution)/shard_map/all_gather | solution.py:115
  77.6 65.1 %all-gather.11.cloned.1.call-done = bf16[4096,128]{1,0:T(8,128)(2,1)} async-done(((bf16[128,128]{1,0:T(8,128)(2,1)}), bf16[4096,128]{1,0:T(8,128)(2,1)}) %all-gather.11.cloned.1.call-update) | async-done | bytes 1048592 | tf_op jit(solution)/shard_map/all_gather | solution.py:117
  142.7 64.0 %all-gather.13.cloned.1.call-done = bf16[4096,128]{0,1:T(8,128)(2,1)} async-done(((bf16[128,128]{0,1:T(8,128)(2,1)}), bf16[4096,128]{0,1:T(8,128)(2,1)}) %all-gather.13.cloned.1.call-update) | async-done | bytes 1048592 | tf_op jit(solution)/shard_map/all_gather | solution.py:116
  206.8 62.7 %all-gather.15.cloned.1.call-done = bf16[4096,128]{0,1:T(8,128)(2,1)} async-done(((bf16[128,128]{0,1:T(8,128)(2,1)}), bf16[4096,128]{0,1:T(8,128)(2,1)}) %all-gather.15.cloned.1.call-update) | async-done | bytes 1048592 | tf_op jit(solution)/shard_map/all_gather | solution.py:118
  269.5 79.9 %while.24 = (s32[]{:T(128)}, f32[128,1,8]{0,2,1:T(8,128)S(1)}, f32[128,1,8]{0,2,1:T(8,128)S(1)}, f32[128,1,8]{0,2,1:T(8,128)S(1)}, f32[128,1,8,128]{0,3,2,1:T(8,...) while((s32[]{:T(128)}, f32[128,1,8]{0,2,1:T(8,128)S(1)}, ...), condition=%wide.region_6.7_spmd.clone, body=%wide.region_1.6_spmd.clone.sunk | while | flops 820517504 | bytes 21996940 | solution.py:79
  269.7 1.3 fusion.71
  271.1 1.4 fusion.69
  272.4 1.9 fusion.72
  274.9 1.6 convolution_bitcast_fusion.4
  276.5 1.6 fusion.74
  278.1 1.3 fusion.75
  279.7 1.3 fusion.71
  281.1 1.4 fusion.69
  282.4 1.9 fusion.72
  284.9 1.6 convolution_bitcast_fusion.4
  286.5 1.6 fusion.74
  288.1 1.3 fusion.75
  289.7 1.3 fusion.71
  291.0 1.4 fusion.69
  292.4 1.9 fusion.72
  294.9 1.6 convolution_bitcast_fusion.4
  296.5 1.6 fusion.74
  298.1 1.3 fusion.75
  299.7 1.3 fusion.71
  301.0 1.4 fusion.69
  302.4 1.9 fusion.72
  304.9 1.6 convolution_bitcast_fusion.4
  306.5 1.6 fusion.74
  308.1 1.3 fusion.75
  309.7 1.3 fusion.71
  311.0 1.4 fusion.69
  312.4 1.9 fusion.72
  314.9 1.6 convolution_bitcast_fusion.4
  316.4 1.6 fusion.74
  318.1 1.3 fusion.75
  319.7 1.3 fusion.71
  321.0 1.4 fusion.69
  322.4 1.9 fusion.72
  324.9 1.6 convolution_bitcast_fusion.4
  326.4 1.6 fusion.74
  328.1 1.3 fusion.75
  329.6 1.3 fusion.71
  331.0 1.4 fusion.69
  332.4 1.9 fusion.72
  334.8 1.6 convolution_bitcast_fusion.4
  336.4 1.6 fusion.74
  338.0 1.3 fusion.75
  339.6 1.3 fusion.71
  341.0 1.4 fusion.69
  342.4 1.9 fusion.72
  344.8 1.6 convolution_bitcast_fusion.4
  346.4 1.6 fusion.74
  348.0 1.3 fusion.75
  349.3 0.8 multiply_reduce_fusion
  350.1 75.8 %psum.7 = f32[]{:T(128)} all-reduce(f32[]{:T(128)} %get-tuple-element.449), channel_id=1, replica_groups=mesh['ctx'=32,'head'=8] {'ctx','head'}, use_global_device_ids=true, to_apply=%region_8.9 | all-reduce | flops 1 | bytes 8 | tf_op jit(solution)/shard_map/psum | solution.py:123
  426.6 0.9 copy.43
  427.4 0.8 copy.42
  (87 shorter events, 6.9 us)
Async XLA Ops:
  7.2 7.3 %copy-start = (s32[32]{0:T(128)S(1)}, s32[32]{0:T(128)}, u32[]{:S(2)}) copy-start(s32[32]{0:T(128)} %param.15) | copy-start | bytes 388
  7.2 70.4 %all-gather.9.cloned.1.call-start = ((), (), s32[]{:S(2)}) async-start(), calls=%async_computation | async-start | bytes 1081344 | tf_op jit(solution)/shard_map/all_gather | solution.py:115
  7.9 134.8 %all-gather.11.cloned.1.call-start = ((), (), s32[]{:S(2)}) async-start(), calls=%async_computation.1 | async-start | bytes 1081344 | tf_op jit(solution)/shard_map/all_gather | solution.py:117
  8.7 198.1 %all-gather.13.cloned.1.call-start = ((), (), s32[]{:S(2)}) async-start(), calls=%async_computation.2 | async-start | bytes 1081344 | tf_op jit(solution)/shard_map/all_gather | solution.py:116
  10.2 259.2 %all-gather.15.cloned.1.call-start = ((), (), s32[]{:S(2)}) async-start(), calls=%async_computation.3 | async-start | bytes 1081344 | tf_op jit(solution)/shard_map/all_gather | solution.py:118
Sparse Core Ops, SparseCore 0:
  9.8 67.7 all-gather.8
  79.4 63.2 all-gather.10
  145.1 61.6 all-gather.12
  209.0 60.4 all-gather.14
where the time goes:
time: 437 us; the launch traced here: 436 us
  waiting for transfers between devices  255 us (58%)
  blocking collectives  75.8 us (17%)
  matrix products  72.6 us (17%)
  between operations  16.3 us (4%)
  other arithmetic  7.76 us (2%)
  local copies, waits for them, and re-layouts  7.28 us (2%)
    psum x1, blocking collectives, shards(): total_squares = lax.psum(square_sum, ('ctx', 'head'))  75.8 us
    all_gather x1, waiting for transfers between devices, shards(): lax.all_gather(dk_three, 'ctx', axis=0, tiled=True)  65.1 us
    all_gather x1, waiting for transfers between devices, shards(): lax.all_gather(v_three, 'ctx', axis=0, tiled=True)  64 us
    all_gather x1, waiting for transfers between devices, shards(): lax.all_gather(dv_three, 'ctx', axis=0, tiled=True)  62.7 us
    all_gather x1, waiting for transfers between devices, shards(): lax.all_gather(k_three, 'ctx', axis=0, tiled=True)  61.9 us
    dot_general x8, matrix products, attend(): jnp.einsum('tghd,sgd->tghs', query_block, ktan_block, preferred_element_t...  15.4 us
    dot_general x8, matrix products, attend(): jnp.einsum('tghs,sgd->tghd', low_weights, value_block, preferred_element_...  13 us
    dot_general x8, matrix products, attend(): jnp.einsum('tghs,sgd->tghd', low_weights, vtan_block, preferred_element_t...  12.5 us
  transfers between devices with their start and end apart: 4, of which 4 were waited for; matrix products, arithmetic and copies ran while one was open for 1% of the time, Pallas kernels for 0%

commit v1 on v0

--- a/solution.py
+++ b/solution.py
@@ -120,7 +120,8 @@
         jnp.int32(0),
     )
     attended, probe_out, square_sum = finish(final, width)
-    total_squares = lax.psum(square_sum, ("ctx", "head"))
+    parts = lax.all_gather(square_sum, ("ctx", "head"), axis=0, tiled=False)
+    total_squares = parts.sum(axis=0)
     entries = row_count * width * count * lax.axis_size("head")
     probe_norm = jnp.sqrt(total_squares / entries)
     return (attended, probe_out, probe_norm)

time: 437 us -> 445 us (1.018)
  matrix products: 72.6 us -> 79.8 us
    psum x1 -> x0, blocking collectives: 75.8 us -> none  [shards(): total_squares = lax.psum(square_sum, ('ctx', 'head'))]
    unnamed x0 -> x1, blocking collectives: none -> 75.5 us
    dot_general x8, matrix products: 13 us -> 20.4 us  [attend(): jnp.einsum('tghs,sgd->tghd', low_weights, value_block, preferred_element_...]
where the time goes in v1:
time: 445 us; the launch traced here: 444 us
  waiting for transfers between devices  254 us (57%)
  matrix products  79.8 us (18%)
  blocking collectives  75.5 us (17%)
  between operations  16.3 us (4%)
  other arithmetic  9.38 us (2%)
  local copies, waits for them, and re-layouts  8.04 us (2%)
    unnamed x1, blocking collectives  75.5 us
    all_gather x1, waiting for transfers between devices, shards(): lax.all_gather(dk_three, 'ctx', axis=0, tiled=True)  65 us
    all_gather x1, waiting for transfers between devices, shards(): lax.all_gather(k_three, 'ctx', axis=0, tiled=True)  64 us
    all_gather x1, waiting for transfers between devices, shards(): lax.all_gather(dv_three, 'ctx', axis=0, tiled=True)  62.8 us
    all_gather x1, waiting for transfers between devices, shards(): lax.all_gather(v_three, 'ctx', axis=0, tiled=True)  61 us
    dot_general x8, matrix products, attend(): jnp.einsum('tghs,sgd->tghd', low_weights, value_block, preferred_element_...  20.4 us
    dot_general x8, matrix products, attend(): jnp.einsum('tghd,sgd->tghs', query_block, ktan_block, preferred_element_t...  15.2 us
    dot_general x8, matrix products, attend(): jnp.einsum('tghs,sgd->tghd', low_weights, vtan_block, preferred_element_t...  12.5 us
  transfers between devices with their start and end apart: 4, of which 4 were waited for; matrix products, arithmetic and copies ran while one was open for 1% of the time, Pallas kernels for 0%

profile of v1, /device:TPU:1, one launch (start us, length us, event | category | flops | bytes accessed | tf_op | source)
XLA Modules:
  0.0 444.0 jit_solution(7224180549734315628)
XLA Ops:
  7.2 1.5 copy.33
  8.8 1.5 copy.34
  10.3 0.7 all-gather.9.cloned.1.call-update
  11.6 1.1 copy.31
  13.0 1.1 copy.32
  14.3 0.6 fusion.42
  15.4 61.0 %all-gather.13.cloned.1.call-done = bf16[4096,128]{0,1:T(8,128)(2,1)} async-done(((bf16[128,128]{0,1:T(8,128)(2,1)}), bf16[4096,128]{0,1:T(8,128)(2,1)}) %all-gather.13.cloned.1.call-update) | async-done | bytes 1048592 | tf_op jit(solution)/shard_map/all_gather | solution.py:116
  76.5 62.8 %all-gather.15.cloned.1.call-done = bf16[4096,128]{0,1:T(8,128)(2,1)} async-done(((bf16[128,128]{0,1:T(8,128)(2,1)}), bf16[4096,128]{0,1:T(8,128)(2,1)}) %all-gather.15.cloned.1.call-update) | async-done | bytes 1048592 | tf_op jit(solution)/shard_map/all_gather | solution.py:118
  139.3 64.0 %all-gather.9.cloned.1.call-done = bf16[4096,128]{1,0:T(8,128)(2,1)} async-done(((bf16[128,128]{1,0:T(8,128)(2,1)}), bf16[4096,128]{1,0:T(8,128)(2,1)}) %all-gather.9.cloned.1.call-update) | async-done | bytes 1048592 | tf_op jit(solution)/shard_map/all_gather | solution.py:115
  203.3 65.0 %all-gather.11.cloned.1.call-done = bf16[4096,128]{1,0:T(8,128)(2,1)} async-done(((bf16[128,128]{1,0:T(8,128)(2,1)}), bf16[4096,128]{1,0:T(8,128)(2,1)}) %all-gather.11.cloned.1.call-update) | async-done | bytes 1048592 | tf_op jit(solution)/shard_map/all_gather | solution.py:117
  268.3 86.9 %while.24 = (s32[]{:T(128)}, f32[128,1,8]{0,2,1:T(8,128)S(1)}, f32[128,1,8]{0,2,1:T(8,128)S(1)}, f32[128,1,8]{0,2,1:T(8,128)S(1)}, f32[128,1,8,128]{0,3,2,1:T(8,...) while((s32[]{:T(128)}, f32[128,1,8]{0,2,1:T(8,128)S(1)}, ...), condition=%wide.region_6.7_spmd.clone, body=%wide.region_1.6_spmd.clone.sunk | while | flops 820517504 | bytes 21996932 | solution.py:79
  268.5 1.4 fusion.69
  269.9 1.3 fusion.71
  271.3 1.9 fusion.72
  273.2 1.6 convolution_bitcast_fusion.4
  274.7 1.3 fusion.75
  276.0 2.4 fusion.74
  279.2 1.4 fusion.69
  280.6 1.3 fusion.71
  281.9 1.9 fusion.72
  283.9 1.6 convolution_bitcast_fusion.4
  285.4 1.3 fusion.75
  286.7 2.6 fusion.74
  290.1 1.4 fusion.69
  291.5 1.3 fusion.71
  292.8 1.9 fusion.72
  294.7 1.6 convolution_bitcast_fusion.4
  296.3 1.3 fusion.75
  297.6 2.6 fusion.74
  301.0 1.4 fusion.69
  302.4 1.3 fusion.71
  303.7 1.9 fusion.72
  305.6 1.6 convolution_bitcast_fusion.4
  307.2 1.3 fusion.75
  308.5 2.6 fusion.74
  311.9 1.4 fusion.69
  313.3 1.3 fusion.71
  314.6 1.9 fusion.72
  316.5 1.6 convolution_bitcast_fusion.4
  318.1 1.3 fusion.75
  319.4 2.6 fusion.74
  322.8 1.4 fusion.69
  324.2 1.3 fusion.71
  325.5 1.9 fusion.72
  327.4 1.6 convolution_bitcast_fusion.4
  329.0 1.3 fusion.75
  330.3 2.6 fusion.74
  333.7 1.4 fusion.69
  335.1 1.3 fusion.71
  336.4 1.9 fusion.72
  338.3 1.6 convolution_bitcast_fusion.4
  339.9 1.3 fusion.75
  341.2 2.6 fusion.74
  344.6 1.4 fusion.69
  346.0 1.3 fusion.71
  347.3 1.9 fusion.72
  349.2 1.6 convolution_bitcast_fusion.4
  350.8 1.3 fusion.75
  352.1 2.6 fusion.74
  355.2 1.8 multiply_reduce_fusion
  357.1 0.8 dynamic-update-slice
  357.8 75.5 %all-reduce = f32[256]{0:T(256)S(1)} all-reduce(f32[256]{0:T(256)S(1)} %dynamic-update-slice), channel_id=1, replica_groups=mesh['ctx'=32,'head'=8] {'ctx','head'}, use_global_device_ids=true, to_apply=%add | all-reduce | flops 256 | bytes 2048
  434.6 0.9 copy.42
  435.5 0.9 copy.43
  (90 shorter events, 8.0 us)
Async XLA Ops:
  7.2 7.1 %copy-start = (s32[32]{0:T(128)S(1)}, s32[32]{0:T(128)}, u32[]{:S(2)}) copy-start(s32[32]{0:T(128)} %param.15) | copy-start | bytes 388
  7.2 69.3 %all-gather.13.cloned.1.call-start = ((), (), s32[]{:S(2)}) async-start(), calls=%async_computation.2 | async-start | bytes 1081344 | tf_op jit(solution)/shard_map/all_gather | solution.py:116
  8.7 130.6 %all-gather.15.cloned.1.call-start = ((), (), s32[]{:S(2)}) async-start(), calls=%async_computation.3 | async-start | bytes 1081344 | tf_op jit(solution)/shard_map/all_gather | solution.py:118
  10.3 193.0 %all-gather.9.cloned.1.call-start = ((), (), s32[]{:S(2)}) async-start(), calls=%async_computation | async-start | bytes 1081344 | tf_op jit(solution)/shard_map/all_gather | solution.py:115
  11.0 257.3 %all-gather.11.cloned.1.call-start = ((), (), s32[]{:S(2)}) async-start(), calls=%async_computation.1 | async-start | bytes 1081344 | tf_op jit(solution)/shard_map/all_gather | solution.py:117
Sparse Core Ops, SparseCore 0:
  10.3 66.0 all-gather.12
  78.8 60.4 all-gather.14
  141.1 62.0 all-gather.8
  205.0 63.2 all-gather.10

commit v2 on v0

--- a/solution.py
+++ b/solution.py
@@ -120,7 +120,8 @@
         jnp.int32(0),
     )
     attended, probe_out, square_sum = finish(final, width)
-    total_squares = lax.psum(square_sum, ("ctx", "head"))
+    apply_series_all = lambda buf: jax.lax.psum(jax.lax.psum(buf, "head"), "ctx")
+    total_squares = apply_series_all(square_sum)
     entries = row_count * width * count * lax.axis_size("head")
     probe_norm = jnp.sqrt(total_squares / entries)
     return (attended, probe_out, probe_norm)

time: 437 us -> 439 us (level)
    psum x1 -> x2, blocking collectives: 75.8 us -> 78 us  [the longest x1 57.1 us: shards(): jax.lax.psum(jax.lax.psum(buf, 'head'), 'ctx')]
where the time goes in v2:
time: 439 us; the launch traced here: 438 us
  waiting for transfers between devices  255 us (58%)
  blocking collectives  78 us (18%)
  matrix products  72.6 us (17%)
  between operations  16.3 us (4%)
  other arithmetic  7.76 us (2%)
  local copies, waits for them, and re-layouts  7.28 us (2%)
    all_gather x1, waiting for transfers between devices, shards(): lax.all_gather(dk_three, 'ctx', axis=0, tiled=True)  65.1 us
    all_gather x1, waiting for transfers between devices, shards(): lax.all_gather(v_three, 'ctx', axis=0, tiled=True)  64 us
    all_gather x1, waiting for transfers between devices, shards(): lax.all_gather(dv_three, 'ctx', axis=0, tiled=True)  62.7 us
    all_gather x1, waiting for transfers between devices, shards(): lax.all_gather(k_three, 'ctx', axis=0, tiled=True)  61.9 us
    psum x1, blocking collectives, shards(): jax.lax.psum(jax.lax.psum(buf, 'head'), 'ctx')  57.1 us
    psum x1, blocking collectives, shards(): jax.lax.psum(buf, 'head')  20.9 us
    dot_general x8, matrix products, attend(): jnp.einsum('tghd,sgd->tghs', query_block, ktan_block, preferred_element_t...  15.4 us
    dot_general x8, matrix products, attend(): jnp.einsum('tghs,sgd->tghd', low_weights, value_block, preferred_element_...  13 us
  transfers between devices with their start and end apart: 4, of which 4 were waited for; matrix products, arithmetic and copies ran while one was open for 1% of the time, Pallas kernels for 0%

profile of v2, /device:TPU:1, one launch (start us, length us, event | category | flops | bytes accessed | tf_op | source)
XLA Modules:
  0.0 438.2 jit_solution(3702050877883943730)
XLA Ops:
  7.2 0.7 all-gather.9.cloned.1.call-update
  8.0 0.7 all-gather.11.cloned.1.call-update
  8.7 1.5 copy.33
  10.3 1.5 copy.34
  11.8 1.1 copy.31
  13.1 1.1 copy.32
  15.7 61.9 %all-gather.9.cloned.1.call-done = bf16[4096,128]{1,0:T(8,128)(2,1)} async-done(((bf16[128,128]{1,0:T(8,128)(2,1)}), bf16[4096,128]{1,0:T(8,128)(2,1)}) %all-gather.9.cloned.1.call-update) | async-done | bytes 1048592 | tf_op jit(solution)/shard_map/all_gather | solution.py:115
  77.6 65.1 %all-gather.11.cloned.1.call-done = bf16[4096,128]{1,0:T(8,128)(2,1)} async-done(((bf16[128,128]{1,0:T(8,128)(2,1)}), bf16[4096,128]{1,0:T(8,128)(2,1)}) %all-gather.11.cloned.1.call-update) | async-done | bytes 1048592 | tf_op jit(solution)/shard_map/all_gather | solution.py:117
  142.7 64.0 %all-gather.13.cloned.1.call-done = bf16[4096,128]{0,1:T(8,128)(2,1)} async-done(((bf16[128,128]{0,1:T(8,128)(2,1)}), bf16[4096,128]{0,1:T(8,128)(2,1)}) %all-gather.13.cloned.1.call-update) | async-done | bytes 1048592 | tf_op jit(solution)/shard_map/all_gather | solution.py:116
  206.8 62.7 %all-gather.15.cloned.1.call-done = bf16[4096,128]{0,1:T(8,128)(2,1)} async-done(((bf16[128,128]{0,1:T(8,128)(2,1)}), bf16[4096,128]{0,1:T(8,128)(2,1)}) %all-gather.15.cloned.1.call-update) | async-done | bytes 1048592 | tf_op jit(solution)/shard_map/all_gather | solution.py:118
  269.5 79.9 %while.24 = (s32[]{:T(128)}, f32[128,1,8]{0,2,1:T(8,128)S(1)}, f32[128,1,8]{0,2,1:T(8,128)S(1)}, f32[128,1,8]{0,2,1:T(8,128)S(1)}, f32[128,1,8,128]{0,3,2,1:T(8,...) while((s32[]{:T(128)}, f32[128,1,8]{0,2,1:T(8,128)S(1)}, ...), condition=%wide.region_6.7_spmd.clone, body=%wide.region_1.6_spmd.clone.sunk | while | flops 820517504 | bytes 21996940 | solution.py:79
  269.7 1.3 fusion.71
  271.1 1.4 fusion.69
  272.4 1.9 fusion.72
  274.9 1.6 convolution_bitcast_fusion.4
  276.5 1.6 fusion.74
  278.1 1.3 fusion.75
  279.7 1.3 fusion.71
  281.1 1.4 fusion.69
  282.4 1.9 fusion.72
  284.9 1.6 convolution_bitcast_fusion.4
  286.5 1.6 fusion.74
  288.1 1.3 fusion.75
  289.7 1.3 fusion.71
  291.0 1.4 fusion.69
  292.4 1.9 fusion.72
  294.9 1.6 convolution_bitcast_fusion.4
  296.5 1.6 fusion.74
  298.1 1.3 fusion.75
  299.7 1.3 fusion.71
  301.0 1.4 fusion.69
  302.4 1.9 fusion.72
  304.9 1.6 convolution_bitcast_fusion.4
  306.5 1.6 fusion.74
  308.1 1.3 fusion.75
  309.7 1.3 fusion.71
  311.0 1.4 fusion.69
  312.4 1.9 fusion.72
  314.9 1.6 convolution_bitcast_fusion.4
  316.4 1.6 fusion.74
  318.1 1.3 fusion.75
  319.7 1.3 fusion.71
  321.0 1.4 fusion.69
  322.4 1.9 fusion.72
  324.9 1.6 convolution_bitcast_fusion.4
  326.4 1.6 fusion.74
  328.1 1.3 fusion.75
  329.6 1.3 fusion.71
  331.0 1.4 fusion.69
  332.4 1.9 fusion.72
  334.8 1.6 convolution_bitcast_fusion.4
  336.4 1.6 fusion.74
  338.0 1.3 fusion.75
  339.6 1.3 fusion.71
  341.0 1.4 fusion.69
  342.4 1.9 fusion.72
  344.8 1.6 convolution_bitcast_fusion.4
  346.4 1.6 fusion.74
  348.0 1.3 fusion.75
  349.3 0.8 multiply_reduce_fusion
  350.1 20.9 %psum.14 = f32[]{:T(128)} all-reduce(f32[]{:T(128)} %get-tuple-element.449), channel_id=1, replica_groups=mesh['ctx'=32,'head'=8] {'head'}, use_global_device_ids=true, to_apply=%region_8.9 | all-reduce | flops 1 | bytes 8 | tf_op jit(solution)/shard_map/psum | solution.py:123
  371.0 57.1 %psum.15 = f32[]{:T(128)} all-reduce(f32[]{:T(128)} %psum.14), channel_id=1, replica_groups=mesh['ctx'=32,'head'=8] {'ctx'}, use_global_device_ids=true, to_apply=%region_9.10 | all-reduce | flops 1 | bytes 8 | tf_op jit(solution)/shard_map/psum | solution.py:123
  428.8 0.9 copy.43
  429.7 0.8 copy.42
  (88 shorter events, 7.6 us)
Async XLA Ops:
  7.2 7.3 %copy-start = (s32[32]{0:T(128)S(1)}, s32[32]{0:T(128)}, u32[]{:S(2)}) copy-start(s32[32]{0:T(128)} %param.15) | copy-start | bytes 388
  7.2 70.4 %all-gather.9.cloned.1.call-start = ((), (), s32[]{:S(2)}) async-start(), calls=%async_computation | async-start | bytes 1081344 | tf_op jit(solution)/shard_map/all_gather | solution.py:115
  7.9 134.8 %all-gather.11.cloned.1.call-start = ((), (), s32[]{:S(2)}) async-start(), calls=%async_computation.1 | async-start | bytes 1081344 | tf_op jit(solution)/shard_map/all_gather | solution.py:117
  8.7 198.1 %all-gather.13.cloned.1.call-start = ((), (), s32[]{:S(2)}) async-start(), calls=%async_computation.2 | async-start | bytes 1081344 | tf_op jit(solution)/shard_map/all_gather | solution.py:116
  10.2 259.2 %all-gather.15.cloned.1.call-start = ((), (), s32[]{:S(2)}) async-start(), calls=%async_computation.3 | async-start | bytes 1081344 | tf_op jit(solution)/shard_map/all_gather | solution.py:118
Sparse Core Ops, SparseCore 0:
  9.8 67.7 all-gather.8
  79.4 63.2 all-gather.10
  145.1 61.6 all-gather.12
  209.0 60.4 all-gather.14
